TPU v7x, 256 devices: a whole 4x4x8 slice. The times are simulated.
256 devices in a mesh: stream: 16 (over y, z_hi, core), span: 16 (over z_lo, x).
Axes of the slice: x: 4, y: 4, z: 8 (z_hi: 2, z_lo: 4; z = z_hi * 4 + z_lo), core: 2. Of those that a mesh axis runs over, the one named last changes fastest.
Arguments:
- velocity_modes: bfloat16 [32, 128, 10, 3, 128], P('stream', 'span'), may hold values from -6 to 6
- cell_weight: float32 [32, 128, 10], P('stream', 'span'), may hold values from 0.001 to 0.01
Outputs:
- convection: float32 [128, 128, 128], replicated
All inputs are finite; a program needn't handle non-finite values.
Results may differ from a plain program's by a relative error of at most 0.0085.
Values may be sent and summed in bfloat16 or wider, within the bound.
A program may use at most 64 MiB of HBM per device.

v0:
```python
import jax
import jax.numpy as jnp
from jax import lax
from jax.sharding import PartitionSpec as P


def with_halo(cells, sides, width):
    for axis, dim in sides:
        count = lax.axis_size(axis)
        ends = count - 1
        head = lax.slice_in_dim(cells, 0, width, axis=dim)
        tail = lax.slice_in_dim(cells, cells.shape[dim] - width, cells.shape[dim], axis=dim)
        cells = jnp.concatenate(
            [
                lax.ppermute(tail, axis, [(i, (i + 1) % count) for i in range(ends)]),
                cells,
                lax.ppermute(head, axis, [((i + 1) % count, i) for i in range(ends)]),
            ],
            axis=dim,
        )
    return cells


def gradient(padded):
    core_x = padded[:, 2:-2]
    deriv_x = (8.0 * (core_x[3:-1] - core_x[1:-3]) - (core_x[4:] - core_x[:-4])) / 12.0
    core_y = padded[2:-2]
    deriv_y = (8.0 * (core_y[:, 3:-1] - core_y[:, 1:-3]) - (core_y[:, 4:] - core_y[:, :-4])) / 12.0
    center = padded[2:-2, 2:-2]
    vertical = jnp.pad(center, ((0, 0), (0, 0), (1, 1), (0, 0), (0, 0)))
    deriv_z = 0.5 * (vertical[:, :, 2:] - vertical[:, :, :-2])
    return jnp.stack([deriv_x, deriv_y, deriv_z])


def shards(velocity_modes, cell_weight):
    padded = with_halo(velocity_modes, (("stream", 0), ("span", 1)), 2)
    grads = gradient(padded.astype(jnp.float32))
    width = velocity_modes.shape[-1]
    cells = velocity_modes.shape[0] * velocity_modes.shape[1] * velocity_modes.shape[2]
    phi_half = velocity_modes.reshape(cells, 3, width)
    grad_cells = grads.reshape(3, cells, 3, width)
    grad_high = grad_cells.astype(jnp.bfloat16)
    grad_low = (grad_cells - grad_high.astype(jnp.float32)).astype(jnp.bfloat16)
    weight_cells = cell_weight.reshape(cells)
    test_count = width * width // width
    block_size = min(8, test_count)
    turns = test_count // block_size

    def one_block(turn_index, result):
        test_start = turn_index * block_size
        phi_test = lax.dynamic_slice_in_dim(phi_half, test_start, block_size, 2)
        quad = jnp.einsum("cbi,acbk->acik", phi_test, grad_high, preferred_element_type=jnp.float32)
        quad = quad + jnp.einsum(
            "cbi,acbk->acik", phi_test, grad_low, preferred_element_type=jnp.float32
        )
        quad = (quad * weight_cells[None, :, None, None]).astype(jnp.bfloat16)
        block_terms = jnp.einsum(
            "caj,acik->ijk", phi_half, quad, preferred_element_type=jnp.float32
        )
        return lax.dynamic_update_slice_in_dim(
            result, block_terms, (turn_index * block_size).astype(jnp.int32), 0
        )

    result = jnp.zeros((test_count, width, width), jnp.float32)
    result = lax.fori_loop(0, turns, one_block, result)
    whole = lax.psum(result.reshape(test_count * width, width), ("stream", "span"))
    return whole.reshape(width, width, width)


def solution(mesh):
    placed = (P("stream", "span", None, None, None), P("stream", "span", None))
    return jax.shard_map(shards, mesh=mesh, in_specs=placed, out_specs=P(), check_vma=False)
```

profile of v0, /device:TPU:1, one launch (start us, length us, event | category | flops | bytes accessed | tf_op | source)
XLA Modules:
  0.0 389.1 jit_solution(13698949483575971565)
XLA Ops:
  6.5 10.2 %collective-permute-start = (bf16[2,8,10,3,128]{4,1,3,2,0:T(8,128)(2,1)}, bf16[2,8,10,3,128]{4,1,3,2,0:T(8,128)(2,1)S(1)}, u32[]{:S(2)}, u32[]{:S(2)}) collective-permute-start(bf16[2,8,10,3,128]{4,1,3,2,0:T(8,128)(2,1)} %param.4), channel_id=1, source_target_pairs={{0,16},{16,32},{32,48},{48,64},{64,80},{80,96},{96,112},{112,128},... | collective-permute-start | bytes 368648 | tf_op jit(solution)/shard_map/ppermute | solution.py:15
  16.7 1.9 collective-permute-start.1
  18.7 1.5 collective-permute-done
  20.2 0.9 constant_dynamic-update-slice_fusion.2
  21.1 6.0 %collective-permute-done.1 = bf16[2,8,10,3,128]{4,1,3,2,0:T(8,128)(2,1)S(1)} collective-permute-done((bf16[2,8,10,3,128]{4,1,3,2,0:T(8,128)(2,1)}, bf16[2,8,10,3,128]{4,1,3,2,0:T(8,128)(2,1)S(1)}, u32[]{:S(2)}, u32[]{:S(2)}) %collective-permute-start.1) | collective-permute-done | bytes 122912 | tf_op jit(solution)/shard_map/ppermute | solution.py:17
  27.3 3.1 collective-permute-start.2
  30.4 1.3 collective-permute-start.3
  31.7 0.9 copy.8
  32.7 0.8 mul.67
  33.5 2.2 collective-permute-done.3
  37.2 4.5 %broadcast_in_dim.3.clone = f32[128,128,128]{2,1,0:T(8,128)} broadcast(f32[]{:T(128)} %constant.37.clone.1), dimensions={} | broadcast | bytes 8388612 | tf_op jit(solution)/shard_map/broadcast_in_dim | solution.py:64
  41.6 55.6 %while.14 = (s32[]{:T(128)}, f32[128,128,128]{2,1,0:T(8,128)}, bf16[160,3,128]{2,0,1:T(8,128)(2,1)S(1)}, bf16[3,160,3,128]{3,2,1,0:T(4,128)(2,1)S(1)}, bf16[3,16...) while((s32[]{:T(128)}, f32[128,128,128]{2,1,0:T(8,128)}, ...), condition=%wide.wide.region_1.2_spmd, body=%wide.wide.region_0.1_spmd.sunk | while | flops 133201928 | bytes 11377443 | solution.py:65
  41.7 0.6 fusion.45
  42.3 0.6 fusion.44
  42.9 1.2 convolution_bitcast_fusion.3
  44.2 0.8 constant_dynamic-update-slice_fusion.6
  46.4 1.2 convolution_bitcast_fusion.3
  47.7 0.8 constant_dynamic-update-slice_fusion.6
  49.8 1.2 convolution_bitcast_fusion.3
  51.2 0.8 constant_dynamic-update-slice_fusion.6
  53.3 1.2 convolution_bitcast_fusion.3
  54.7 0.8 constant_dynamic-update-slice_fusion.6
  56.8 1.2 convolution_bitcast_fusion.3
  58.1 0.8 constant_dynamic-update-slice_fusion.6
  60.2 1.2 convolution_bitcast_fusion.3
  61.6 0.8 constant_dynamic-update-slice_fusion.6
  63.7 1.2 convolution_bitcast_fusion.3
  65.1 0.8 constant_dynamic-update-slice_fusion.6
  67.2 1.2 convolution_bitcast_fusion.3
  68.6 0.8 constant_dynamic-update-slice_fusion.6
  70.7 1.2 convolution_bitcast_fusion.3
  72.0 0.8 constant_dynamic-update-slice_fusion.6
  74.1 1.2 convolution_bitcast_fusion.3
  75.5 0.8 constant_dynamic-update-slice_fusion.6
  77.6 1.2 convolution_bitcast_fusion.3
  79.0 0.8 constant_dynamic-update-slice_fusion.6
  81.1 1.2 convolution_bitcast_fusion.3
  82.4 0.8 constant_dynamic-update-slice_fusion.6
  84.6 1.2 convolution_bitcast_fusion.3
  85.9 0.8 constant_dynamic-update-slice_fusion.6
  88.0 1.2 convolution_bitcast_fusion.3
  89.4 0.8 constant_dynamic-update-slice_fusion.6
  91.5 1.2 convolution_bitcast_fusion.3
  92.9 0.8 constant_dynamic-update-slice_fusion.6
  95.0 1.2 convolution_bitcast_fusion.3
  96.3 0.8 constant_dynamic-update-slice_fusion.6
  97.2 277.2 %all-reduce.3.cloned.1.call-done = f32[128,128,128]{2,1,0:T(8,128)} async-done(((f32[128,128,128]{2,1,0:T(8,128)}), f32[128,128,128]{2,1,0:T(8,128)}) %all-reduce.3.cloned.1.call-update) | async-done | bytes 8388624 | tf_op jit(solution)/shard_map/psum | solution.py:66
  374.4 7.9 %copy.73 = f32[128,128,128]{2,1,0:T(8,128)} copy(f32[128,128,128]{2,1,0:T(8,128)} %all-reduce.3.cloned.1.call-done) | data formatting | bytes 16777216
  (77 shorter events, 23.7 us)
Async XLA Ops:
  6.5 367.8 %all-reduce.3.cloned.1.call-start = ((), (), s32[]{:S(2)}) async-start(), calls=%async_computation | async-start | bytes 16777216 | tf_op jit(solution)/shard_map/psum | solution.py:66
  6.5 13.6 %collective-permute-start = (bf16[2,8,10,3,128]{4,1,3,2,0:T(8,128)(2,1)}, bf16[2,8,10,3,128]{4,1,3,2,0:T(8,128)(2,1)S(1)}, u32[]{:S(2)}, u32[]{:S(2)}) collective-permute-start(bf16[2,8,10,3,128]{4,1,3,2,0:T(8,128)(2,1)} %param.4), channel_id=1, source_target_pairs={{0,16},{16,32},{32,48},{48,64},{64,80},{80,96},{96,112},{112,128},... | collective-permute-start | bytes 368648 | tf_op jit(solution)/shard_map/ppermute | solution.py:15
  16.7 10.4 %collective-permute-start.1 = (bf16[2,8,10,3,128]{4,1,3,2,0:T(8,128)(2,1)}, bf16[2,8,10,3,128]{4,1,3,2,0:T(8,128)(2,1)S(1)}, u32[]{:S(2)}, u32[]{:S(2)}) collective-permute-start(bf16[2,8,10,3,128]{4,1,3,2,0:T(8,128)(2,1)} %param.4), channel_id=1, source_target_pairs={{16,0},{32,16},{48,32},{64,48},{80,64},{96,80},{112,96},{128,112},... | collective-permute-start | bytes 368648 | tf_op jit(solution)/shard_map/ppermute | solution.py:17
  27.3 6.2 %collective-permute-start.2 = (bf16[6,2,10,3,128]{4,1,3,2,0:T(2,128)(2,1)S(1)}, bf16[6,2,10,3,128]{4,1,3,2,0:T(2,128)(2,1)S(1)}, u32[]{:S(2)}, u32[]{:S(2)}) collective-permute-start(bf16[6,2,10,3,128]{4,1,3,2,0:T(2,128)(2,1)S(1)} %get-tuple-element.130), channel_id=1, source_target_pairs={{0,1},{1,2},{2,3},{3,4},{4,5},{5,6},{6,7},{7,8},{8,9},{9,10},{10,1... | collective-permute-start | bytes 276488 | tf_op jit(solution)/shard_map/ppermute | solution.py:15
  30.4 5.3 %collective-permute-start.3 = (bf16[6,2,10,3,128]{4,1,3,2,0:T(2,128)(2,1)S(1)}, bf16[6,2,10,3,128]{4,1,3,2,0:T(2,128)(2,1)S(1)}, u32[]{:S(2)}, u32[]{:S(2)}) collective-permute-start(bf16[6,2,10,3,128]{4,1,3,2,0:T(2,128)(2,1)S(1)} %get-tuple-element.131), channel_id=1, source_target_pairs={{1,0},{2,1},{3,2},{4,3},{5,4},{6,5},{7,6},{8,7},{9,8},{10,9},{11,1... | collective-permute-start | bytes 276488 | tf_op jit(solution)/shard_map/ppermute | solution.py:17
Sparse Core Ops, SparseCore 0:
  97.3 277.0 all-reduce.2
where the time goes:
time: 390 us; the launch traced here: 389 us
  waiting for transfers between devices  287 us (74%)
  matrix products  36.9 us (9%)
  local copies, waits for them, and re-layouts  33.7 us (9%)
  starting transfers between devices  16.5 us (4%)
  between operations  13.5 us (3%)
    psum x1, waiting for transfers between devices, shards(): lax.psum(result.reshape(test_count * width, width), ('stream', 'span'))  277 us
    dot_general x16, matrix products, one_block(): jnp.einsum('caj,acik->ijk', phi_half, quad, preferred_element_type=jnp.fl...  18.4 us
    dynamic_update_slice x32, local copies, waits for them, and re-layouts, one_block(): lax.dynamic_update_slice_in_dim(result, block_terms, (turn_index * block_...  16.6 us
    ppermute x2, starting transfers between devices, with_halo(): lax.ppermute(tail, axis, [(i, (i + 1) % count) for i in range(ends)])  13.3 us
    unnamed x4, local copies, waits for them, and re-layouts  9.77 us
    dot_general x16, matrix products, one_block(): jnp.einsum('cbi,acbk->acik', phi_test, grad_high, preferred_element_type=...  9.23 us
    dot_general x16, matrix products, one_block(): jnp.einsum('cbi,acbk->acik', phi_test, grad_low, preferred_element_type=j...  9.22 us
    ppermute x2, waiting for transfers between devices, with_halo(): lax.ppermute(head, axis, [((i + 1) % count, i) for i in range(ends)])  8.23 us
  transfers between devices with their start and end apart: 5, of which 4 were waited for; matrix products, arithmetic and copies ran while one was open for 1% of the time, Pallas kernels for 0%

commit v1 on v0

v1 whole, which is shorter than its diff:
```python
import jax
import jax.numpy as jnp
from jax import lax
from jax.experimental import pallas as pl
from jax.experimental.pallas import tpu as pltpu
from jax.sharding import PartitionSpec as P

MESH = pl.DeviceIdType.MESH
F32, BF16 = jnp.float32, jnp.bfloat16
M = 128
NX, NY, NZ = 2, 8, 10
CELLS = NX * NY * NZ
HALF = M // 2
ROWS = HALF * M
CX, CY, CZH, CZL = 4, 4, 2, 4
CZ = CZH * CZL
VMEM = pl.BlockSpec(memory_space=pltpu.VMEM)


def coords():
    s, p = lax.axis_index("stream"), lax.axis_index("span")
    core = lax.rem(s, 2)
    zh = lax.rem(s // 2, CZH)
    y = s // (2 * CZH)
    zl = p // CX
    x = lax.rem(p, CX)
    return x, y, zh * CZL + zl, core


def device(x, y, z, core):
    return ((y * CZH + z // CZL) * 2 + core, lax.rem(z, CZL) * CX + x)


def halo_kernel(phi_ref, w_ref, x_ref, halo, ext, send_sem, recv_sem):
    s, p = lax.axis_index("stream"), lax.axis_index("span")
    ns, np_ = lax.axis_size("stream"), lax.axis_size("span")
    core = lax.rem(s, 2)
    partner = (s + 1 - 2 * core, p)
    before, after = (lax.rem(s + ns - 1, ns), p), (lax.rem(s + 1, ns), p)
    left, right = (s, lax.rem(p + np_ - 1, np_)), (s, lax.rem(p + 1, np_))

    barrier = pltpu.get_barrier_semaphore()
    for peer in (before, after, left, right):
        pl.semaphore_signal(barrier, inc=1, device_id=peer, device_id_type=MESH)
    pl.semaphore_wait(barrier, 4)

    copies = []
    for slot, peer in ((1, before), (0, after), (3, left), (2, right)):
        copy = pltpu.make_async_remote_copy(
            src_ref=phi_ref,
            dst_ref=halo.at[slot],
            send_sem=send_sem.at[slot],
            recv_sem=recv_sem.at[slot],
            device_id=peer,
            device_id_type=MESH,
        )
        copy.start()
        copies.append(copy)
    from_after, from_before, from_right, from_left = copies[0], copies[1], copies[2], copies[3]

    def weight(x, z):
        return jnp.broadcast_to(w_ref[x, :, z : z + 1], (NY, M))

    def rows(x, z):
        return pl.ds((x * NZ + z) * NY, NY)

    zero = jnp.zeros((NY, M), F32)

    def own(x, z, b):
        return phi_ref[x, z, b].astype(F32)

    for x in range(NX):
        for z in range(NZ):
            for b in range(3):
                x_ref[b, core, rows(x, z), :] = phi_ref[x, z, b]
                up = own(x, z + 1, b) if z + 1 < NZ else zero
                down = own(x, z - 1, b) if z > 0 else zero
                grad = 0.5 * (up - down) * weight(x, z)
                x_ref[9 + b, core, rows(x, z), :] = grad.astype(BF16)

    from_left.wait()
    from_right.wait()
    has_left = (p > 0).astype(F32)
    has_right = (p < np_ - 1).astype(F32)
    for x in range(NX):
        for z in range(NZ):
            for b in range(3):
                ext[0:NY] = halo[2, x, z, b].astype(F32) * has_left
                ext[NY : 2 * NY] = own(x, z, b)
                ext[2 * NY : 3 * NY] = halo[3, x, z, b].astype(F32) * has_right
                near = ext[NY + 1 : 2 * NY + 1] - ext[NY - 1 : 2 * NY - 1]
                far = ext[NY + 2 : 2 * NY + 2] - ext[NY - 2 : 2 * NY - 2]
                grad = (8.0 * near - far) * (weight(x, z) * (1.0 / 12.0))
                x_ref[6 + b, core, rows(x, z), :] = grad.astype(BF16)

    def to_partner(k, first, count):
        copy = pltpu.make_async_remote_copy(
            src_ref=x_ref.at[pl.ds(first, count), core],
            dst_ref=x_ref.at[pl.ds(first, count), core],
            send_sem=send_sem.at[k],
            recv_sem=recv_sem.at[k],
            device_id=partner,
            device_id_type=MESH,
        )
        copy.start()
        return copy

    pair = [to_partner(4, 0, 3), to_partner(5, 6, 6)]

    from_before.wait()
    from_after.wait()
    has_before = (s > 0).astype(F32)
    has_after = (s < ns - 1).astype(F32)
    for z in range(NZ):
        for b in range(3):
            a0 = halo[0, 0, z, b].astype(F32) * has_before
            a1 = halo[0, 1, z, b].astype(F32) * has_before
            c0, c1 = own(0, z, b), own(1, z, b)
            d0 = halo[1, 0, z, b].astype(F32) * has_after
            d1 = halo[1, 1, z, b].astype(F32) * has_after
            g0 = (8.0 * (c1 - a1) - (d0 - a0)) * (weight(0, z) * (1.0 / 12.0))
            g1 = (8.0 * (d0 - c0) - (d1 - a1)) * (weight(1, z) * (1.0 / 12.0))
            x_ref[3 + b, core, rows(0, z), :] = g0.astype(BF16)
            x_ref[3 + b, core, rows(1, z), :] = g1.astype(BF16)
    pair.append(to_partner(6, 3, 3))
    for copy in pair:
        copy.wait()


def halo_call(phi, weight):
    return pl.pallas_call(
        halo_kernel,
        out_shape=jax.ShapeDtypeStruct((12, 2, CELLS, M), BF16),
        in_specs=[VMEM, VMEM],
        out_specs=VMEM,
        scratch_shapes=[
            pltpu.VMEM((4, NX, NZ, 3, NY, M), BF16),
            pltpu.VMEM((3 * NY, M), F32),
            pltpu.SemaphoreType.DMA((7,)),
            pltpu.SemaphoreType.DMA((7,)),
        ],
        compiler_params=pltpu.CompilerParams(collective_id=0, has_side_effects=True),
        name="halo",
    )(phi, weight)


BLOCK = 4
TILES = 8


def product_kernel(x_ref, out_ref, phi_i, grad, test, quad_a, quad_b):
    core = lax.rem(lax.axis_index("stream"), 2)
    flat = x_ref

    def piece(q, first, count):
        dev, row = first // CELLS, first % CELLS
        if row + count <= CELLS:
            return flat[q, dev, row : row + count, :]
        head = CELLS - row
        return jnp.concatenate(
            [flat[q, dev, row:CELLS, :], flat[q, dev + 1, 0 : count - head, :]], axis=0
        )

    def tile(base, stride, t):
        if t < 6:
            return piece(base + stride * (t // 2), (t % 2) * M, M)
        if t == 6:
            return jnp.concatenate(
                [piece(base, 2 * M, 64), piece(base + stride, 2 * M, 64)], axis=0
            )
        return jnp.concatenate(
            [piece(base + 2 * stride, 2 * M, 64), jnp.zeros((64, M), BF16)], axis=0
        )

    for t in range(TILES):
        test[t * M : (t + 1) * M, :] = tile(0, 1, t)
        for b in range(3):
            grad[b, t] = tile(3 + b, 3, t).astype(F32).T
    for b in range(3):
        for half in range(3):
            if half < 2:
                cells = piece(b, half * M, M)
            else:
                tail = piece(b, 2 * M, 64)
                cells = jnp.concatenate([tail, tail], axis=0)
            phi_i[b, half] = cells.astype(F32).T

    def quads(block, quad):
        for t in range(TILES):
            half = t % 2 if t < 6 else 2
            for n in range(BLOCK):
                i = core * HALF + block * BLOCK + n
                q = phi_i[0, half, pl.ds(i, 1), :] * grad[0, t]
                q = q + phi_i[1, half, pl.ds(i, 1), :] * grad[1, t]
                q = q + phi_i[2, half, pl.ds(i, 1), :] * grad[2, t]
                quad[n * M : (n + 1) * M, t * M : (t + 1) * M] = q.astype(BF16)

    def contract(block, quad):
        res = jnp.dot(quad[...], test[...], preferred_element_type=F32)
        for n in range(BLOCK):
            first = pl.multiple_of((block * BLOCK + n) * M, M)
            out_ref[pl.ds(first, M), :] = res[n * M : (n + 1) * M].T.astype(BF16)

    blocks = HALF // BLOCK
    quads(0, quad_a)

    @pl.loop(0, blocks // 2 - 1)
    def _(turn):
        quads(2 * turn + 1, quad_b)
        contract(2 * turn, quad_a)
        quads(2 * turn + 2, quad_a)
        contract(2 * turn + 1, quad_b)

    quads(blocks - 1, quad_b)
    contract(blocks - 2, quad_a)
    contract(blocks - 1, quad_b)


def product_call(gathered):
    return pl.pallas_call(
        product_kernel,
        out_shape=jax.ShapeDtypeStruct((ROWS, M), BF16),
        in_specs=[VMEM],
        out_specs=VMEM,
        scratch_shapes=[
            pltpu.VMEM((3, 3, M, M), F32),
            pltpu.VMEM((3, TILES, M, M), F32),
            pltpu.VMEM((TILES * M, M), BF16),
            pltpu.VMEM((BLOCK * M, TILES * M), BF16),
            pltpu.VMEM((BLOCK * M, TILES * M), BF16),
        ],
        name="product",
    )(gathered)


CHUNKS = 4
CH = ROWS // CHUNKS
N1, N2, N3 = CH // 4, CH // 16, CH // 128


def sum_kernel(part_ref, full_ref, got1, got2, got3, sum1, sum2, send_sem, recv_sem):
    x, y, z, core = coords()
    u = x * (1 - core) + y * core
    v = y * (1 - core) + x * core

    def along_u(d):
        return device(lax.rem(x + d * (1 - core), CX), lax.rem(y + d * core, CY), z, core)

    def along_v(d):
        return device(lax.rem(x + d * core, CX), lax.rem(y + d * (1 - core), CY), z, core)

    def along_z(d):
        return device(x, y, lax.rem(z + d, CZ), core)

    partner = device(x, y, z, 1 - core)
    barrier = pltpu.get_barrier_semaphore()
    peers = [along_u(d) for d in (1, 2, 3)] + [along_v(d) for d in (1, 2, 3)]
    peers += [along_z(d) for d in range(1, CZ)] + [partner]
    for peer in peers:
        pl.semaphore_signal(barrier, inc=1, device_id=peer, device_id_type=MESH)
    pl.semaphore_wait(barrier, len(peers))

    def send(src, dst, c, k, peer):
        copy = pltpu.make_async_remote_copy(
            src_ref=src,
            dst_ref=dst,
            send_sem=send_sem.at[c, k],
            recv_sem=recv_sem.at[c, k],
            device_id=peer,
            device_id_type=MESH,
        )
        copy.start()
        return copy

    flying = {}

    def block(first, count):
        return pl.ds(pl.multiple_of(first, count), count)

    def stage0(c):
        flying[c, 0] = [
            send(
                part_ref.at[block(c * CH + lax.rem(u + d, 4) * N1, N1)],
                got1.at[c, d - 1],
                c,
                d - 1,
                along_u(d),
            )
            for d in (2, 1, 3)
        ]

    def stage1(c):
        for copy in flying[c, 0]:
            copy.wait()
        total = part_ref[block(c * CH + u * N1, N1), :].astype(F32)
        for d in range(3):
            total = total + got1[c, d].astype(F32)
        sum1[c] = total.astype(BF16)
        flying[c, 1] = [
            send(
                sum1.at[c, block(lax.rem(v + d, 4) * N2, N2)], got2.at[c, d - 1], c, 2 + d, along_v(d)
            )
            for d in (2, 1, 3)
        ]

    def stage2(c):
        for copy in flying[c, 1]:
            copy.wait()
        total = sum1[c, block(v * N2, N2), :].astype(F32)
        for d in range(3):
            total = total + got2[c, d].astype(F32)
        sum2[c] = total.astype(BF16)
        flying[c, 2] = [
            send(
                sum2.at[c, block(lax.rem(z + d, CZ) * N3, N3)], got3.at[c, d - 1], c, 5 + d, along_z(d)
            )
            for d in (4, 3, 5, 2, 6, 1, 7)
        ]

    def mine(c, uu, vv, zz):
        return c * CH + uu * N1 + vv * N2 + zz * N3

    def stage3(c):
        for copy in flying[c, 2]:
            copy.wait()
        total = sum2[c, block(z * N3, N3), :].astype(F32)
        for d in range(CZ - 1):
            total = total + got3[c, d].astype(F32)
        shard = full_ref.at[core, block(mine(c, u, v, z), N3)]
        full_ref[core, block(mine(c, u, v, z), N3), :] = total.astype(BF16)
        flying[c, 3] = [send(shard, shard, c, 12 + d, along_z(d)) for d in (4, 3, 5, 2, 6, 1, 7)]

    def stage4(c):
        for copy in flying[c, 3]:
            copy.wait()
        piece = full_ref.at[core, block(mine(c, u, v, 0), N2)]
        flying[c, 4] = [send(piece, piece, c, 19 + d, along_v(d)) for d in (2, 1, 3)]

    def stage5(c):
        for copy in flying[c, 4]:
            copy.wait()
        piece = full_ref.at[core, block(mine(c, u, 0, 0), N1)]
        flying[c, 5] = [send(piece, piece, c, 22 + d, along_u(d)) for d in (2, 1, 3)]

    def stage6(c):
        for copy in flying[c, 5]:
            copy.wait()
        piece = full_ref.at[core, pl.ds(c * CH, CH)]
        flying[c, 6] = [send(piece, piece, c, 26, partner)]

    def stage7(c):
        for copy in flying[c, 6]:
            copy.wait()

    stages = [stage0, stage1, stage2, stage3, stage4, stage5, stage6, stage7]
    for turn in range(CHUNKS + len(stages) - 1):
        for k in reversed(range(len(stages))):
            if 0 <= turn - k < CHUNKS:
                stages[k](turn - k)


def sum_call(part):
    return pl.pallas_call(
        sum_kernel,
        out_shape=jax.ShapeDtypeStruct((2, ROWS, M), BF16),
        in_specs=[VMEM],
        out_specs=VMEM,
        scratch_shapes=[
            pltpu.VMEM((CHUNKS, 3, N1, M), BF16),
            pltpu.VMEM((CHUNKS, 3, N2, M), BF16),
            pltpu.VMEM((CHUNKS, CZ - 1, N3, M), BF16),
            pltpu.VMEM((CHUNKS, N1, M), BF16),
            pltpu.VMEM((CHUNKS, N2, M), BF16),
            pltpu.SemaphoreType.DMA((CHUNKS, 27)),
            pltpu.SemaphoreType.DMA((CHUNKS, 27)),
        ],
        compiler_params=pltpu.CompilerParams(collective_id=1, has_side_effects=True),
        name="sum",
    )(part)


def shards(velocity_modes, cell_weight):
    phi = jnp.transpose(velocity_modes, (0, 2, 3, 1, 4))
    gathered = halo_call(phi, cell_weight)
    part = product_call(gathered)
    full = sum_call(part)
    return full.reshape(M, M, M).astype(F32)


def solution(mesh):
    placed = (P("stream", "span", None, None, None), P("stream", "span", None))
    return jax.shard_map(shards, mesh=mesh, in_specs=placed, out_specs=P(), check_vma=False)
```

time: 390 us -> 104 us (0.27)
  waiting for transfers between devices: 287 us -> 0 us
  Pallas kernels: 0 us -> 97.5 us
  matrix products: 36.9 us -> 0 us
  local copies, waits for them, and re-layouts: 33.7 us -> 0 us
  starting transfers between devices: 16.5 us -> 0 us
  between operations: 13.5 us -> 0.02 us
  other arithmetic: 1.12 us -> 6.66 us
    psum x1 -> x0, waiting for transfers between devices: 277 us -> none  [shards(): lax.psum(result.reshape(test_count * width, width), ('stream', 'span'))]
    pallas_call x0 -> x3, Pallas kernels: none -> 97.5 us  [the longest x1 58.5 us: sum_call(): pl.pallas_call(sum_kernel, out_shape=jax.ShapeDtypeStruct((2, ROWS, M), B...]
    dot_general x48 -> x0, matrix products: 36.9 us -> none  [the longest x16 18.4 us: one_block(): jnp.einsum('caj,acik->ijk', phi_half, quad, preferred_element_type=jnp.fl...]
    dynamic_update_slice x32 -> x0, local copies, waits for them, and re-layouts: 16.6 us -> none  [one_block(): lax.dynamic_update_slice_in_dim(result, block_terms, (turn_index * block_...]
    ppermute x4 -> x0, starting transfers between devices: 16.5 us -> none  [the longest x2 13.3 us: with_halo(): lax.ppermute(tail, axis, [(i, (i + 1) % count) for i in range(ends)])]
    unnamed x4 -> x0, local copies, waits for them, and re-layouts: 9.77 us -> none
    ppermute x4 -> x0, waiting for transfers between devices: 9.74 us -> none  [the longest x2 8.23 us: with_halo(): lax.ppermute(head, axis, [((i + 1) % count, i) for i in range(ends)])]
    convert_element_type x3 -> x1, other arithmetic: 0.92 us -> 6.66 us  [shards(): return full.reshape(M, M, M).astype(F32)]
  transfers between devices with their start and end apart: 5 -> 0, of which waited for: 4 -> 0; matrix products, arithmetic and copies ran while one was open for 1% -> 0% of each run, Pallas kernels for 0% -> 0%
where the time goes in v1:
time: 104 us
  Pallas kernels  97.5 us (94%)
  other arithmetic  6.66 us (6%)
    pallas_call x1, Pallas kernels, sum_call(): pl.pallas_call(sum_kernel, out_shape=jax.ShapeDtypeStruct((2, ROWS, M), B...  58.5 us
    pallas_call x1, Pallas kernels, halo_call(): pl.pallas_call(halo_kernel, out_shape=jax.ShapeDtypeStruct((12, 2, CELLS,...  24.7 us
    pallas_call x1, Pallas kernels, product_call(): pl.pallas_call(product_kernel, out_shape=jax.ShapeDtypeStruct((ROWS, M),...  14.2 us
    convert_element_type x1, other arithmetic, shards(): return full.reshape(M, M, M).astype(F32)  6.66 us

profile of v1, /device:TPU:1, one launch (start us, length us, event | category | flops | bytes accessed | tf_op | source)
XLA Modules:
  0.0 104.2 jit_solution(12602500271530037341)
XLA Ops:
  0.0 24.7 %halo.1.x_ref = bf16[12,2,160,128]{3,2,1,0:T(8,128)(2,1)} custom-call(bf16[2,10,3,8,128]{4,3,2,1,0:T(8,128)(2,1)} %bitcast.4, f32[2,8,10]{2,1,0:T(8,128)} %w_ref.1), custom_call_target="tpu_custom_call" | custom-call | tf_op jit(solution)/shard_map/halo/pallas_call | solution.py:131
  24.8 14.2 %product.1.part_ref = bf16[8192,128]{1,0:T(8,128)(2,1)} custom-call(bf16[12,2,160,128]{3,2,1,0:T(8,128)(2,1)} %halo.1.x_ref), custom_call_target="tpu_custom_call" | custom-call | tf_op jit(solution)/shard_map/product/pallas_call | solution.py:220
  39.0 58.5 %sum.1 = bf16[2,8192,128]{2,1,0:T(8,128)(2,1)} custom-call(bf16[8192,128]{1,0:T(8,128)(2,1)} %product.1.part_ref), custom_call_target="tpu_custom_call" | custom-call | tf_op jit(solution)/shard_map/sum/pallas_call | solution.py:363
  97.5 6.7 %convert.1 = f32[128,128,128]{2,1,0:T(8,128)} convert(bf16[128,128,128]{2,1,0:T(8,128)(2,1)} %bitcast.3) | non-fusion elementwise | flops 2097152 | bytes 12582912 | tf_op jit(solution)/shard_map/convert_element_type | solution.py:387

commit v2 on v1

v2 whole, which is shorter than its diff:
```python
import jax
import jax.numpy as jnp
from jax import lax
from jax.experimental import pallas as pl
from jax.experimental.pallas import tpu as pltpu
from jax.sharding import PartitionSpec as P

MESH = pl.DeviceIdType.MESH
F32, BF16 = jnp.float32, jnp.bfloat16
M = 128
NX, NY, NZ = 2, 8, 10
CELLS = NX * NY * NZ
HALF = M // 2
ROWS = HALF * M
CX, CY, CZH, CZL = 4, 4, 2, 4
CZ = CZH * CZL
VMEM = pl.BlockSpec(memory_space=pltpu.VMEM)


def coords():
    s, p = lax.axis_index("stream"), lax.axis_index("span")
    core = lax.rem(s, 2)
    zh = lax.rem(s // 2, CZH)
    y = s // (2 * CZH)
    zl = p // CX
    x = lax.rem(p, CX)
    return x, y, zh * CZL + zl, core


def device(x, y, z, core):
    return ((y * CZH + z // CZL) * 2 + core, lax.rem(z, CZL) * CX + x)


def halo_kernel(phi_ref, w_ref, x_ref, halo, ext, send_sem, recv_sem):
    s, p = lax.axis_index("stream"), lax.axis_index("span")
    ns, np_ = lax.axis_size("stream"), lax.axis_size("span")
    core = lax.rem(s, 2)
    partner = (s + 1 - 2 * core, p)
    before, after = (lax.rem(s + ns - 1, ns), p), (lax.rem(s + 1, ns), p)
    left, right = (s, lax.rem(p + np_ - 1, np_)), (s, lax.rem(p + 1, np_))

    barrier = pltpu.get_barrier_semaphore()
    for peer in (before, after, left, right):
        pl.semaphore_signal(barrier, inc=1, device_id=peer, device_id_type=MESH)
    pl.semaphore_wait(barrier, 4)

    copies = []
    for slot, peer in ((1, before), (0, after), (3, left), (2, right)):
        copy = pltpu.make_async_remote_copy(
            src_ref=phi_ref,
            dst_ref=halo.at[slot],
            send_sem=send_sem.at[slot],
            recv_sem=recv_sem.at[slot],
            device_id=peer,
            device_id_type=MESH,
        )
        copy.start()
        copies.append(copy)
    from_after, from_before, from_right, from_left = copies[0], copies[1], copies[2], copies[3]

    def weight(x, z):
        return jnp.broadcast_to(w_ref[x, :, z : z + 1], (NY, M))

    def rows(x, z):
        return pl.ds((x * NZ + z) * NY, NY)

    zero = jnp.zeros((NY, M), F32)

    def own(x, z, b):
        return phi_ref[x, z, b].astype(F32)

    for x in range(NX):
        for z in range(NZ):
            for b in range(3):
                x_ref[b, core, rows(x, z), :] = phi_ref[x, z, b]
                up = own(x, z + 1, b) if z + 1 < NZ else zero
                down = own(x, z - 1, b) if z > 0 else zero
                grad = 0.5 * (up - down) * weight(x, z)
                x_ref[9 + b, core, rows(x, z), :] = grad.astype(BF16)

    from_left.wait()
    from_right.wait()
    has_left = (p > 0).astype(F32)
    has_right = (p < np_ - 1).astype(F32)
    for x in range(NX):
        for z in range(NZ):
            for b in range(3):
                ext[0:NY] = halo[2, x, z, b].astype(F32) * has_left
                ext[NY : 2 * NY] = own(x, z, b)
                ext[2 * NY : 3 * NY] = halo[3, x, z, b].astype(F32) * has_right
                near = ext[NY + 1 : 2 * NY + 1] - ext[NY - 1 : 2 * NY - 1]
                far = ext[NY + 2 : 2 * NY + 2] - ext[NY - 2 : 2 * NY - 2]
                grad = (8.0 * near - far) * (weight(x, z) * (1.0 / 12.0))
                x_ref[6 + b, core, rows(x, z), :] = grad.astype(BF16)

    def to_partner(k, first, count):
        copy = pltpu.make_async_remote_copy(
            src_ref=x_ref.at[pl.ds(first, count), core],
            dst_ref=x_ref.at[pl.ds(first, count), core],
            send_sem=send_sem.at[k],
            recv_sem=recv_sem.at[k],
            device_id=partner,
            device_id_type=MESH,
        )
        copy.start()
        return copy

    pair = [to_partner(4, 0, 3), to_partner(5, 6, 6)]

    from_before.wait()
    from_after.wait()
    has_before = (s > 0).astype(F32)
    has_after = (s < ns - 1).astype(F32)
    for z in range(NZ):
        for b in range(3):
            a0 = halo[0, 0, z, b].astype(F32) * has_before
            a1 = halo[0, 1, z, b].astype(F32) * has_before
            c0, c1 = own(0, z, b), own(1, z, b)
            d0 = halo[1, 0, z, b].astype(F32) * has_after
            d1 = halo[1, 1, z, b].astype(F32) * has_after
            g0 = (8.0 * (c1 - a1) - (d0 - a0)) * (weight(0, z) * (1.0 / 12.0))
            g1 = (8.0 * (d0 - c0) - (d1 - a1)) * (weight(1, z) * (1.0 / 12.0))
            x_ref[3 + b, core, rows(0, z), :] = g0.astype(BF16)
            x_ref[3 + b, core, rows(1, z), :] = g1.astype(BF16)
    pair.append(to_partner(6, 3, 3))
    for copy in pair:
        copy.wait()


def halo_call(phi, weight):
    return pl.pallas_call(
        halo_kernel,
        out_shape=jax.ShapeDtypeStruct((12, 2, CELLS, M), BF16),
        in_specs=[VMEM, VMEM],
        out_specs=VMEM,
        scratch_shapes=[
            pltpu.VMEM((4, NX, NZ, 3, NY, M), BF16),
            pltpu.VMEM((3 * NY, M), F32),
            pltpu.SemaphoreType.DMA((7,)),
            pltpu.SemaphoreType.DMA((7,)),
        ],
        compiler_params=pltpu.CompilerParams(
            collective_id=0, has_side_effects=True, vmem_limit_bytes=16 * 2**20
        ),
        name="halo",
    )(phi, weight)


BLOCK = 4
TILES = 8
PACK = 16
CHUNKS = (16, 16, 16, 16)
ORDER = (
    (-1, 0), (0, 0), (-1, 1), (0, 1), (-1, 2), (1, 0), (0, 2), (-1, 3), (1, 1), (0, 3), (1, 2), (2, 0),
    (1, 3), (2, 1), (3, 0), (2, 2), (3, 1), (2, 3), (3, 2), (4, 0), (3, 3), (4, 1), (5, 0), (4, 2),
    (6, 0), (5, 1), (4, 3), (5, 2), (6, 1), (6, 2), (5, 3), (6, 3),
)
COPIES = 3 + 7 + 3 + 7 + 3 + 1


def tensor_kernel(
    x_ref, full_ref, part, got1, sum1, got2, shard, phi_t, grad, test, quad_a, quad_b, send_sem, recv_sem
):
    x, y, z, core = coords()
    u = x * (1 - core) + y * core
    v = y * (1 - core) + x * core

    def along_u(d):
        return device(lax.rem(x + d * (1 - core), CX), lax.rem(y + d * core, CY), z, core)

    def along_v(d):
        return device(lax.rem(x + d * core, CX), lax.rem(y + d * (1 - core), CY), z, core)

    def along_z(d):
        return device(x, y, lax.rem(z + d, CZ), core)

    partner = device(x, y, z, 1 - core)
    barrier = pltpu.get_barrier_semaphore()
    peers = [along_u(d) for d in (1, 2, 3)] + [along_v(d) for d in (1, 2, 3)]
    peers += [along_z(d) for d in range(1, CZ)] + [partner]
    for peer in peers:
        pl.semaphore_signal(barrier, inc=1, device_id=peer, device_id_type=MESH)


    def piece(q, first, count):
        dev, row = first // CELLS, first % CELLS
        if row + count <= CELLS:
            return x_ref[q, dev, row : row + count, :]
        head = CELLS - row
        return jnp.concatenate(
            [x_ref[q, dev, row:CELLS, :], x_ref[q, dev + 1, 0 : count - head, :]], axis=0
        )

    def tile(base, stride, t):
        if t < 6:
            return piece(base + stride * (t // 2), (t % 2) * M, M)
        if t == 6:
            return jnp.concatenate(
                [piece(base, 2 * M, 64), piece(base + stride, 2 * M, 64)], axis=0
            )
        return jnp.concatenate(
            [piece(base + 2 * stride, 2 * M, 64), jnp.zeros((64, M), BF16)], axis=0
        )

    for t in range(TILES):
        test[t * M // PACK : (t + 1) * M // PACK] = tile(0, 1, t).reshape(M // PACK, PACK, M)
        for b in range(3):
            grad[b, t] = tile(3 + b, 3, t).astype(F32).T
    for b in range(3):
        for half in range(3):
            if half < 2:
                cells = piece(b, half * M, M)
            else:
                tail = piece(b, 2 * M, 64)
                cells = jnp.concatenate([tail, tail], axis=0)
            phi_t[b, half] = cells.astype(F32).T

    def quads(block, quad):
        first = core * HALF + block * BLOCK

        def row(n, b, half):
            wide = jnp.broadcast_to(phi_t[b, half, pl.ds(first + n, 1), :], (PACK, M))
            return wide.astype(BF16)

        for t in range(TILES):
            half = t % 2 if t < 6 else 2
            phi = [[row(n, b, half) for b in range(3)] for n in range(BLOCK)]
            for k in range(0, M, PACK):
                g = [grad[b, t, k : k + PACK, :].astype(BF16) for b in range(3)]
                for n in range(BLOCK):
                    q = phi[n][0] * g[0] + phi[n][1] * g[1] + phi[n][2] * g[2]
                    quad[t, (n * M + k) // PACK] = q

    def contract(block, quad):
        left = jnp.concatenate([quad[t].reshape(BLOCK * M, M) for t in range(TILES)], axis=1)
        res = jnp.dot(left, test[...].reshape(TILES * M, M), preferred_element_type=F32)
        for n in range(BLOCK):
            first = pl.multiple_of((block * BLOCK + n) * M, M)
            part[pl.ds(first, M), :] = res[n * M : (n + 1) * M].T.astype(BF16)

    def two_blocks(turn, more):
        quads(2 * turn + 1, quad_b)
        contract(2 * turn, quad_a)
        if more:
            quads(2 * turn + 2, quad_a)
        contract(2 * turn + 1, quad_b)

    starts = [sum(CHUNKS[:c]) for c in range(len(CHUNKS))]

    def compute(c):
        last = c == len(CHUNKS) - 1
        begin, end = starts[c] // (2 * BLOCK), (starts[c] + CHUNKS[c]) // (2 * BLOCK)
        if c == 0:
            quads(0, quad_a)

        @pl.loop(begin, end - 1 if last else end)
        def _(turn):
            two_blocks(turn, True)

        if last:
            two_blocks(end - 1, False)


    flying = {}

    def send(c, k, src, dst, peer):
        copy = pltpu.make_async_remote_copy(
            src_ref=src,
            dst_ref=dst,
            send_sem=send_sem.at[c, k],
            recv_sem=recv_sem.at[c, k],
            device_id=peer,
            device_id_type=MESH,
        )
        copy.start()
        flying.setdefault(c, []).append(copy)

    def wait(c):
        for copy in flying.pop(c):
            copy.wait()

    def rows(first, count):
        return pl.ds(pl.multiple_of(first, count), count)

    def at1(c):
        return starts[c] * M // 4

    def at2(c):
        return starts[c] * M // 32

    def stage(k, c):
        n0 = CHUNKS[c] * M
        n1, n2 = n0 // 4, n0 // 32
        first = starts[c] * M
        part_row = lambda uu: pl.ds(pl.multiple_of(first + uu * n1, n2), n1)
        full_row = lambda uu, zz: pl.ds(pl.multiple_of(first + uu * n1 + zz * n2, n2), n2)
        if k > 0:
            wait(c)
        if k == 0:
            for d in (2, 1, 3):
                there = lax.rem(u + d, 4)
                send(c, d - 1, part.at[part_row(there)], got1.at[d - 1, pl.ds(at1(c), n1)], along_u(d))
        if k == 1:
            total = part[part_row(u), :].astype(F32)
            for d in range(3):
                total = total + got1[d, at1(c) : at1(c) + n1, :].astype(F32)
            sum1[at1(c) : at1(c) + n1, :] = total.astype(BF16)
            for d in (4, 3, 5, 2, 6, 1, 7):
                there = lax.rem(z + d, CZ)
                send(
                    c, 2 + d,
                    sum1.at[pl.ds(pl.multiple_of(at1(c) + there * n2, n2), n2)],
                    got2.at[d - 1, pl.ds(at2(c), n2)],
                    along_z(d),
                )
        if k == 2:
            total = sum1[pl.ds(pl.multiple_of(at1(c) + z * n2, n2), n2), :].astype(F32)
            for d in range(CZ - 1):
                total = total + got2[d, at2(c) : at2(c) + n2, :].astype(F32)
            shard[v, at2(c) : at2(c) + n2, :] = total.astype(BF16)
            mine = shard.at[v, pl.ds(at2(c), n2)]
            for d in (2, 1, 3):
                send(c, 9 + d, mine, mine, along_v(d))
        if k == 3:
            total = shard[0, at2(c) : at2(c) + n2, :].astype(F32)
            for d in range(1, 4):
                total = total + shard[d, at2(c) : at2(c) + n2, :].astype(F32)
            full_ref[core, full_row(u, z), :] = total.astype(BF16)
            mine = full_ref.at[core, full_row(u, z)]
            for d in (4, 3, 5, 2, 6, 1, 7):
                send(c, 12 + d, mine, mine, along_z(d))
        if k == 4:
            mine = full_ref.at[core, part_row(u)]
            for d in (2, 1, 3):
                send(c, 19 + d, mine, mine, along_u(d))
        if k == 5:
            mine = full_ref.at[core, pl.ds(first, n0)]
            send(c, 23, mine, mine, partner)

    for k, c in ORDER:
        if k < 0:
            compute(c)
            if c == 0:
                pl.semaphore_wait(barrier, len(peers))
        else:
            stage(k, c)


def tensor_call(gathered):
    return pl.pallas_call(
        tensor_kernel,
        out_shape=jax.ShapeDtypeStruct((2, ROWS, M), BF16),
        in_specs=[VMEM],
        out_specs=VMEM,
        scratch_shapes=[
            pltpu.VMEM((ROWS, M), BF16),
            pltpu.VMEM((3, ROWS // 4, M), BF16),
            pltpu.VMEM((ROWS // 4, M), BF16),
            pltpu.VMEM((CZ - 1, ROWS // 32, M), BF16),
            pltpu.VMEM((4, ROWS // 32, M), BF16),
            pltpu.VMEM((3, 3, M, M), F32),
            pltpu.VMEM((3, TILES, M, M), F32),
            pltpu.VMEM((TILES * M // PACK, PACK, M), BF16),
            pltpu.VMEM((TILES, BLOCK * M // PACK, PACK, M), BF16),
            pltpu.VMEM((TILES, BLOCK * M // PACK, PACK, M), BF16),
            pltpu.SemaphoreType.DMA((len(CHUNKS), COPIES)),
            pltpu.SemaphoreType.DMA((len(CHUNKS), COPIES)),
        ],
        compiler_params=pltpu.CompilerParams(
            collective_id=1, has_side_effects=True, vmem_limit_bytes=32 * 2**20
        ),
        name="tensor",
    )(gathered)


def shards(velocity_modes, cell_weight):
    phi = jnp.transpose(velocity_modes, (0, 2, 3, 1, 4))
    gathered = halo_call(phi, cell_weight)
    full = tensor_call(gathered)
    return full.reshape(M, M, M).astype(F32)


def solution(mesh):
    placed = (P("stream", "span", None, None, None), P("stream", "span", None))
    return jax.shard_map(shards, mesh=mesh, in_specs=placed, out_specs=P(), check_vma=False)
```

time: 104 us -> 74.2 us (0.71)
  Pallas kernels: 97.5 us -> 68 us
  other arithmetic: 6.66 us -> 4.45 us
  local copies, waits for them, and re-layouts: 0 us -> 1.6 us
    pallas_call x2 -> x1, Pallas kernels: 72.8 us -> 45.1 us  [tensor_call(): pl.pallas_call(tensor_kernel, out_shape=jax.ShapeDtypeStruct((2, ROWS, M)...]
    convert_element_type x1, other arithmetic: 6.66 us -> 4.45 us  [shards(): return full.reshape(M, M, M).astype(F32)]
    pallas_call x1, Pallas kernels: 24.7 us -> 22.9 us  [halo_call(): pl.pallas_call(halo_kernel, out_shape=jax.ShapeDtypeStruct((12, 2, CELLS,...]
    unnamed x0 -> x4, local copies, waits for them, and re-layouts: none -> 1.6 us
where the time goes in v2:
time: 74.2 us; the launch traced here: 74.1 us
  Pallas kernels  68 us (92%)
  other arithmetic  4.45 us (6%)
  local copies, waits for them, and re-layouts  1.6 us (2%)
    pallas_call x1, Pallas kernels, tensor_call(): pl.pallas_call(tensor_kernel, out_shape=jax.ShapeDtypeStruct((2, ROWS, M)...  45.1 us
    pallas_call x1, Pallas kernels, halo_call(): pl.pallas_call(halo_kernel, out_shape=jax.ShapeDtypeStruct((12, 2, CELLS,...  22.9 us
    convert_element_type x1, other arithmetic, shards(): return full.reshape(M, M, M).astype(F32)  4.45 us
    unnamed x4, local copies, waits for them, and re-layouts  1.6 us

profile of v2, /device:TPU:1, one launch (start us, length us, event | category | flops | bytes accessed | tf_op | source)
XLA Modules:
  0.0 74.1 jit_solution(16136989811269129649)
XLA Ops:
  0.0 0.0 copy-start
  0.0 0.9 %copy-done = bf16[2,8,10,3,128]{4,1,3,2,0:T(8,128)(2,1)S(1)} copy-done((bf16[2,8,10,3,128]{4,1,3,2,0:T(8,128)(2,1)S(1)}, bf16[2,8,10,3,128]{4,1,3,2,0:T(8,128)(2,1)}, u32[]{:S(2)}) %copy-start) | copy-done | bytes 122904
  0.9 0.0 copy-start.1
  0.9 0.7 copy-done.1
  1.6 22.9 %halo.1.x_ref = bf16[12,2,160,128]{3,2,1,0:T(8,128)(2,1)S(1)} custom-call(bf16[2,10,3,8,128]{4,3,2,1,0:T(8,128)(2,1)S(1)} %bitcast.4, f32[2,8,10]{2,1,0:T(8,128)S(1)} %copy-done.1), custom_call_target="tpu_custom_call" | custom-call | tf_op jit(solution)/shard_map/halo/pallas_call | solution.py:131
  24.5 45.1 %tensor.1 = bf16[2,8192,128]{2,1,0:T(8,128)(2,1)S(1)} custom-call(bf16[12,2,160,128]{3,2,1,0:T(8,128)(2,1)S(1)} %halo.1.x_ref), custom_call_target="tpu_custom_call" | custom-call | tf_op jit(solution)/shard_map/tensor/pallas_call | solution.py:350
  69.6 4.4 %convert.1 = f32[128,128,128]{2,1,0:T(8,128)} convert(bf16[128,128,128]{2,1,0:T(8,128)(2,1)S(1)} %bitcast.3) | non-fusion elementwise | flops 2097152 | bytes 12582912 | tf_op jit(solution)/shard_map/convert_element_type | solution.py:380
Async XLA Ops:
  0.0 0.9 %copy-start = (bf16[2,8,10,3,128]{4,1,3,2,0:T(8,128)(2,1)S(1)}, bf16[2,8,10,3,128]{4,1,3,2,0:T(8,128)(2,1)}, u32[]{:S(2)}) copy-start(bf16[2,8,10,3,128]{4,1,3,2,0:T(8,128)(2,1)} %param.2) | copy-start | bytes 368644
  0.9 0.7 copy-start.1

commit v3 on v2

v3 whole, which is shorter than its diff:
```python
import jax
import jax.numpy as jnp
from jax import lax
from jax.experimental import pallas as pl
from jax.experimental.pallas import tpu as pltpu
from jax.sharding import PartitionSpec as P

MESH = pl.DeviceIdType.MESH
F32, BF16 = jnp.float32, jnp.bfloat16
M = 128
NX, NY, NZ = 2, 8, 10
CELLS = NX * NY * NZ
HALF = M // 2
ROWS = HALF * M
CX, CY, CZH, CZL = 4, 4, 2, 4
CZ = CZH * CZL
VMEM = pl.BlockSpec(memory_space=pltpu.VMEM)


def coords():
    s, p = lax.axis_index("stream"), lax.axis_index("span")
    core = lax.rem(s, 2)
    zh = lax.rem(s // 2, CZH)
    y = s // (2 * CZH)
    zl = p // CX
    x = lax.rem(p, CX)
    return x, y, zh * CZL + zl, core


def device(x, y, z, core):
    return ((y * CZH + z // CZL) * 2 + core, lax.rem(z, CZL) * CX + x)


BLOCK = 4
PACK = 16
TILES_YZ, TILES_X = 5, 3
TILES = TILES_YZ + TILES_X
CHUNKS = (16, 16, 16, 16)
ORDER = (
    (-1, 0), (0, 0), (-1, 1), (0, 1), (-1, 2), (1, 0), (0, 2), (-1, 3), (1, 1), (0, 3), (1, 2), (2, 0),
    (1, 3), (2, 1), (3, 0), (2, 2), (3, 1), (2, 3), (3, 2), (4, 0), (3, 3), (4, 1), (5, 0), (4, 2),
    (6, 0), (4, 3), (5, 1), (5, 2), (6, 1), (5, 3), (6, 2), (6, 3),
)
COPIES = 3 + 7 + 3 + 7 + 3 + 4
FAR = 2


def tensor_kernel(
    phi_hbm, w_hbm, full_ref, own, w_ref, halo, ext, xs, part, got1, sum1, got2, shard,
    phi_t, grad, test, quad_a, quad_b, local_sem, halo_send, halo_recv, send_sem, recv_sem,
):
    s, p = lax.axis_index("stream"), lax.axis_index("span")
    ns, np_ = lax.axis_size("stream"), lax.axis_size("span")
    before, after = (lax.rem(s + ns - 1, ns), p), (lax.rem(s + 1, ns), p)
    left, right = (s, lax.rem(p + np_ - 1, np_)), (s, lax.rem(p + 1, np_))
    x, y, z, core = coords()
    u = x * (1 - core) + y * core
    v = y * (1 - core) + x * core

    def along_u(d):
        return device(lax.rem(x + d * (1 - core), CX), lax.rem(y + d * core, CY), z, core)

    def along_v(d):
        return device(lax.rem(x + d * core, CX), lax.rem(y + d * (1 - core), CY), z, core)

    def along_z(d):
        return device(x, y, lax.rem(z + d, CZ), core)

    partner = device(x, y, z, 1 - core)
    barrier = pltpu.get_barrier_semaphore()
    peers = [before, after, left, right, partner]
    peers += [along_u(d) for d in (1, 2, 3)] + [along_v(d) for d in (1, 2, 3)]
    peers += [along_z(d) for d in range(1, CZ)]
    for peer in peers:
        pl.semaphore_signal(barrier, inc=1, device_id=peer, device_id_type=MESH)
    take = [
        pltpu.make_async_copy(phi_hbm, own, local_sem.at[0]),
        pltpu.make_async_copy(w_hbm, w_ref, local_sem.at[1]),
    ]
    for copy in take:
        copy.start()
    pl.semaphore_wait(barrier, len(peers))


    def halo_copy(k, src, dst, peer):
        copy = pltpu.make_async_remote_copy(
            src_ref=src,
            dst_ref=dst,
            send_sem=halo_send.at[k],
            recv_sem=halo_recv.at[k],
            device_id=peer,
            device_id_type=MESH,
        )
        copy.start()
        return copy

    far_halo = []
    for n in range(FAR):
        zs = pl.ds(n * NZ // FAR, NZ // FAR)
        far_halo.append(
            (
                halo_copy(7 + n, phi_hbm.at[:, zs], halo.at[1, :, zs], before),
                halo_copy(7 + FAR + n, phi_hbm.at[:, zs], halo.at[0, :, zs], after),
            )
        )
    from_right = halo_copy(3, phi_hbm, halo.at[3], left)
    from_left = halo_copy(2, phi_hbm, halo.at[2], right)
    for copy in take:
        copy.wait()

    def weight(x, z):
        return jnp.broadcast_to(w_ref[x, :, z : z + 1], (NY, M))

    def cells_at(x, z):
        return pl.ds((x * NZ + z) * NY, NY)

    def here(x, z, b):
        return own[x, z, b].astype(F32)

    def to_partner(k, first, count):
        mine = xs.at[pl.ds(first, count), core]
        return halo_copy(k, mine, mine, partner)

    zero = jnp.zeros((NY, M), F32)
    for x_ in range(NX):
        for z_ in range(NZ):
            for b in range(3):
                xs[b, core, cells_at(x_, z_), :] = own[x_, z_, b]
                up = here(x_, z_ + 1, b) if z_ + 1 < NZ else zero
                down = here(x_, z_ - 1, b) if z_ > 0 else zero
                g = 0.5 * (up - down) * weight(x_, z_)
                xs[9 + b, core, cells_at(x_, z_), :] = g.astype(BF16)
    pair = [to_partner(4, 0, 3), to_partner(5, 9, 3)]

    from_left.wait()
    from_right.wait()
    has_left = (p > 0).astype(F32)
    has_right = (p < np_ - 1).astype(F32)
    for x_ in range(NX):
        for z_ in range(NZ):
            for b in range(3):
                line = ext.at[(x_ * NZ + z_) * 3 + b]
                line[0:NY] = halo[2, x_, z_, b].astype(F32) * has_left
                line[NY : 2 * NY] = here(x_, z_, b)
                line[2 * NY : 3 * NY] = halo[3, x_, z_, b].astype(F32) * has_right
    for x_ in range(NX):
        for z_ in range(NZ):
            for b in range(3):
                line = ext.at[(x_ * NZ + z_) * 3 + b]
                near = line[NY + 1 : 2 * NY + 1] - line[NY - 1 : 2 * NY - 1]
                far = line[NY + 2 : 2 * NY + 2] - line[NY - 2 : 2 * NY - 2]
                g = (8.0 * near - far) * (weight(x_, z_) * (1.0 / 12.0))
                xs[6 + b, core, cells_at(x_, z_), :] = g.astype(BF16)
    pair.append(to_partner(6, 6, 3))
    for copy in pair:
        copy.wait()


    def piece(q, first, count):
        dev, row = first // CELLS, first % CELLS
        if row + count <= CELLS:
            return xs[q, dev, row : row + count, :]
        head = CELLS - row
        return jnp.concatenate(
            [xs[q, dev, row:CELLS, :], xs[q, dev + 1, 0 : count - head, :]], axis=0
        )

    def tile(qx, qy, qz, t):
        if t < 4:
            return piece((qy, qz)[t // 2], (t % 2) * M, M)
        if t == 4:
            return jnp.concatenate([piece(qy, 2 * M, 64), piece(qz, 2 * M, 64)], axis=0)
        if t < 7:
            return piece(qx, (t - 5) * M, M)
        return jnp.concatenate([piece(qx, 2 * M, 64), jnp.zeros((64, M), BF16)], axis=0)

    HALVES = (0, 1, 0, 1, 2, 0, 1, 2)

    def load_grad(t):
        for b in range(3):
            grad[b, t] = tile(3 + b, 6 + b, 9 + b, t).astype(F32).T

    for t in range(TILES):
        test[t * M // PACK : (t + 1) * M // PACK] = tile(0, 1, 2, t).reshape(M // PACK, PACK, M)
    for b in range(3):
        for half in range(3):
            if half < 2:
                cells = piece(b, half * M, M)
            else:
                tail = piece(b, 2 * M, 64)
                cells = jnp.concatenate([tail, tail], axis=0)
            phi_t[b, half] = cells.astype(F32).T
    for t in range(TILES_YZ):
        load_grad(t)


    has_before = (s > 0).astype(F32)
    has_after = (s < ns - 1).astype(F32)
    pair = []
    for n in range(FAR):
        for copy in far_halo[n]:
            copy.wait()
        zs = range(n * NZ // FAR, (n + 1) * NZ // FAR)
        for z_ in zs:
            for b in range(3):
                a0 = halo[0, 0, z_, b].astype(F32) * has_before
                a1 = halo[0, 1, z_, b].astype(F32) * has_before
                c0, c1 = here(0, z_, b), here(1, z_, b)
                d0 = halo[1, 0, z_, b].astype(F32) * has_after
                d1 = halo[1, 1, z_, b].astype(F32) * has_after
                g0 = (8.0 * (c1 - a1) - (d0 - a0)) * (weight(0, z_) * (1.0 / 12.0))
                g1 = (8.0 * (d0 - c0) - (d1 - a1)) * (weight(1, z_) * (1.0 / 12.0))
                xs[3 + b, core, cells_at(0, z_), :] = g0.astype(BF16)
                xs[3 + b, core, cells_at(1, z_), :] = g1.astype(BF16)
        for x_ in range(NX):
            mine = xs.at[pl.ds(3, 3), core, pl.ds((x_ * NZ + zs[0]) * NY, len(zs) * NY)]
            pair.append(halo_copy(7 + 2 * FAR + n * NX + x_, mine, mine, partner))
    for copy in pair:
        copy.wait()
    for t in range(TILES_YZ, TILES):
        load_grad(t)

    def quads(block, quad):
        first = core * HALF + block * BLOCK

        def row(n, b, half):
            wide = jnp.broadcast_to(phi_t[b, half, pl.ds(first + n, 1), :], (PACK, M))
            return wide.astype(BF16)

        for t in range(TILES):
            phi = [[row(n, b, HALVES[t]) for b in range(3)] for n in range(BLOCK)]
            for k in range(0, M, PACK):
                g = [grad[b, t, k : k + PACK, :].astype(BF16) for b in range(3)]
                for n in range(BLOCK):
                    q = phi[n][0] * g[0] + phi[n][1] * g[1] + phi[n][2] * g[2]
                    quad[t, (n * M + k) // PACK] = q

    def contract(block, quad):
        wide = jnp.concatenate([quad[t].reshape(BLOCK * M, M) for t in range(TILES)], axis=1)
        res = jnp.dot(wide, test[...].reshape(TILES * M, M), preferred_element_type=F32)
        for n in range(BLOCK):
            first = pl.multiple_of((block * BLOCK + n) * M, M)
            part[pl.ds(first, M), :] = res[n * M : (n + 1) * M].T.astype(BF16)

    def two_blocks(turn, more):
        quads(2 * turn + 1, quad_b)
        contract(2 * turn, quad_a)
        if more:
            quads(2 * turn + 2, quad_a)
        contract(2 * turn + 1, quad_b)

    turns = HALF // (2 * BLOCK)
    starts = [sum(CHUNKS[:c]) for c in range(len(CHUNKS))]

    def compute(c):
        last = c == len(CHUNKS) - 1
        begin, end = starts[c] // (2 * BLOCK), (starts[c] + CHUNKS[c]) // (2 * BLOCK)
        if c == 0:
            quads(0, quad_a)

        @pl.loop(begin, end - 1 if last else end)
        def _(turn):
            two_blocks(turn, True)

        if last:
            two_blocks(turns - 1, False)


    flying = {}

    def send(c, k, src, dst, peer):
        copy = pltpu.make_async_remote_copy(
            src_ref=src,
            dst_ref=dst,
            send_sem=send_sem.at[c, k],
            recv_sem=recv_sem.at[c, k],
            device_id=peer,
            device_id_type=MESH,
        )
        copy.start()
        flying.setdefault(c, []).append(copy)

    def wait(c):
        for copy in flying.pop(c):
            copy.wait()

    def at1(c):
        return starts[c] * M // 4

    def at2(c):
        return starts[c] * M // 32

    def stage(k, c):
        n0 = CHUNKS[c] * M
        n1, n2 = n0 // 4, n0 // 32
        first = starts[c] * M
        part_row = lambda uu: pl.ds(pl.multiple_of(first + uu * n1, n2), n1)
        full_row = lambda uu, zz: pl.ds(pl.multiple_of(first + uu * n1 + zz * n2, n2), n2)
        if k > 0 and k != 5:
            wait(c)
        if k == 0:
            for d in (2, 1, 3):
                there = lax.rem(u + d, 4)
                send(c, d - 1, part.at[part_row(there)], got1.at[d - 1, pl.ds(at1(c), n1)], along_u(d))
        if k == 1:
            total = part[part_row(u), :].astype(F32)
            for d in range(3):
                total = total + got1[d, at1(c) : at1(c) + n1, :].astype(F32)
            sum1[at1(c) : at1(c) + n1, :] = total.astype(BF16)
            for d in (4, 3, 5, 2, 6, 1, 7):
                there = lax.rem(z + d, CZ)
                send(
                    c, 2 + d,
                    sum1.at[pl.ds(pl.multiple_of(at1(c) + there * n2, n2), n2)],
                    got2.at[d - 1, pl.ds(at2(c), n2)],
                    along_z(d),
                )
        if k == 2:
            total = sum1[pl.ds(pl.multiple_of(at1(c) + z * n2, n2), n2), :].astype(F32)
            for d in range(CZ - 1):
                total = total + got2[d, at2(c) : at2(c) + n2, :].astype(F32)
            shard[v, at2(c) : at2(c) + n2, :] = total
            mine = shard.at[v, pl.ds(at2(c), n2)]
            for d in (2, 1, 3):
                send(c, 9 + d, mine, mine, along_v(d))
        if k == 3:
            total = shard[0, at2(c) : at2(c) + n2, :]
            for d in range(1, 4):
                total = total + shard[d, at2(c) : at2(c) + n2, :]
            full_ref[core, full_row(u, z), :] = total.astype(BF16)
            mine = full_ref.at[core, full_row(u, z)]
            for d in (4, 3, 5, 2, 6, 1, 7):
                send(c, 12 + d, mine, mine, along_z(d))
        if k == 4:
            mine = full_ref.at[core, part_row(u)]
            for d in (2, 1, 3):
                send(c, 19 + d, mine, mine, along_u(d))
            send(c, 23, mine, mine, partner)
        if k == 5:
            two, one, three, own_piece = flying.pop(c)
            for d, copy in ((1, one), (3, three), (2, two)):
                copy.wait()
                piece_u = full_ref.at[core, part_row(lax.rem(u + 4 - d, 4))]
                send(c, 23 + d, piece_u, piece_u, partner)
            flying[c].append(own_piece)

    for k, c in ORDER:
        if k < 0:
            compute(c)
        else:
            stage(k, c)


def tensor_call(phi, weight):
    return pl.pallas_call(
        tensor_kernel,
        out_shape=jax.ShapeDtypeStruct((2, ROWS, M), BF16),
        in_specs=[pl.BlockSpec(memory_space=pltpu.MemorySpace.HBM)] * 2,
        out_specs=VMEM,
        scratch_shapes=[
            pltpu.VMEM((NX, NZ, 3, NY, M), BF16),
            pltpu.VMEM((NX, NY, NZ), F32),
            pltpu.VMEM((4, NX, NZ, 3, NY, M), BF16),
            pltpu.VMEM((NX * NZ * 3, 3 * NY, M), F32),
            pltpu.VMEM((12, 2, CELLS, M), BF16),
            pltpu.VMEM((ROWS, M), BF16),
            pltpu.VMEM((3, ROWS // 4, M), BF16),
            pltpu.VMEM((ROWS // 4, M), BF16),
            pltpu.VMEM((CZ - 1, ROWS // 32, M), BF16),
            pltpu.VMEM((4, ROWS // 32, M), F32),
            pltpu.VMEM((3, 3, M, M), F32),
            pltpu.VMEM((3, TILES, M, M), F32),
            pltpu.VMEM((TILES * M // PACK, PACK, M), BF16),
            pltpu.VMEM((TILES, BLOCK * M // PACK, PACK, M), BF16),
            pltpu.VMEM((TILES, BLOCK * M // PACK, PACK, M), BF16),
            pltpu.SemaphoreType.DMA((2,)),
            pltpu.SemaphoreType.DMA((7 + 4 * FAR,)),
            pltpu.SemaphoreType.DMA((7 + 4 * FAR,)),
            pltpu.SemaphoreType.DMA((len(CHUNKS), COPIES)),
            pltpu.SemaphoreType.DMA((len(CHUNKS), COPIES)),
        ],
        compiler_params=pltpu.CompilerParams(
            collective_id=0, has_side_effects=True, vmem_limit_bytes=40 * 2**20
        ),
        name="tensor",
    )(pltpu.with_memory_space_constraint(phi, pltpu.HBM), pltpu.with_memory_space_constraint(weight, pltpu.HBM))


PARTS = 16


def widen_kernel(src_ref, out_ref, wide, sem):
    count = M * M // PARTS
    copies = []
    for n in range(PARTS):
        wide[n * count : (n + 1) * count, :] = src_ref[n * count : (n + 1) * count, :].astype(F32)
        span = pl.ds(n * count, count)
        copy = pltpu.make_async_copy(wide.at[span], out_ref.at[span], sem.at[n])
        copy.start()
        copies.append(copy)
    for copy in copies:
        copy.wait()


def widen_call(full):
    return pl.pallas_call(
        widen_kernel,
        out_shape=jax.ShapeDtypeStruct((M * M, M), F32),
        in_specs=[VMEM],
        out_specs=pl.BlockSpec(memory_space=pl.ANY),
        scratch_shapes=[pltpu.VMEM((M * M, M), F32), pltpu.SemaphoreType.DMA((PARTS,))],
        compiler_params=pltpu.CompilerParams(vmem_limit_bytes=24 * 2**20),
        name="widen",
    )(full)


def shards(velocity_modes, cell_weight):
    phi = jnp.transpose(velocity_modes, (0, 2, 3, 1, 4))
    full = tensor_call(phi, cell_weight)
    return widen_call(full.reshape(M * M, M)).reshape(M, M, M)


def solution(mesh):
    placed = (P("stream", "span", None, None, None), P("stream", "span", None))
    return jax.shard_map(shards, mesh=mesh, in_specs=placed, out_specs=P(), check_vma=False)
```

time: 74.2 us -> 71.7 us (0.966)
  other arithmetic: 4.45 us -> 0 us
  Pallas kernels: 68 us -> 71.6 us
  local copies, waits for them, and re-layouts: 1.6 us -> 0 us
    pallas_call x1, Pallas kernels: 45.1 us -> 68.2 us  [tensor_call(): pl.pallas_call(tensor_kernel, out_shape=jax.ShapeDtypeStruct((2, ROWS, M)...]
    pallas_call x1, Pallas kernels: 22.9 us -> 3.45 us  [widen_call(): pl.pallas_call(widen_kernel, out_shape=jax.ShapeDtypeStruct((M * M, M), F...]
    convert_element_type x1 -> x0, other arithmetic: 4.45 us -> none  [shards(): return full.reshape(M, M, M).astype(F32)]
    unnamed x4 -> x0, local copies, waits for them, and re-layouts: 1.6 us -> none
where the time goes in v3:
time: 71.7 us; the launch traced here: 71.6 us
  Pallas kernels  71.6 us (100%)
    pallas_call x1, Pallas kernels, tensor_call(): pl.pallas_call(tensor_kernel, out_shape=jax.ShapeDtypeStruct((2, ROWS, M)...  68.2 us
    pallas_call x1, Pallas kernels, widen_call(): pl.pallas_call(widen_kernel, out_shape=jax.ShapeDtypeStruct((M * M, M), F...  3.45 us

profile of v3, /device:TPU:1, one launch (start us, length us, event | category | flops | bytes accessed | tf_op | source)
XLA Modules:
  0.0 71.6 jit_solution(15441676995257400690)
XLA Ops:
  0.0 68.2 %tensor.1 = bf16[2,8192,128]{2,1,0:T(8,128)(2,1)S(1)} custom-call(bf16[2,10,3,8,128]{4,3,2,1,0:T(8,128)(2,1)} %bitcast.4, f32[2,8,10]{2,1,0:T(8,128)} %w_hbm.1), custom_call_target="tpu_custom_call" | custom-call | tf_op jit(solution)/shard_map/tensor/pallas_call | solution.py:355
  68.2 3.5 %widen.1 = f32[16384,128]{1,0:T(8,128)} custom-call(bf16[16384,128]{1,0:T(8,128)(2,1)S(1)} %bitcast.3), custom_call_target="tpu_custom_call" | custom-call | tf_op jit(solution)/shard_map/widen/pallas_call | solution.py:406

commit v4 on v3

--- a/solution.py
+++ b/solution.py
@@ -37,9 +37,9 @@
 TILES = TILES_YZ + TILES_X
 CHUNKS = (16, 16, 16, 16)
 ORDER = (
-    (-1, 0), (0, 0), (-1, 1), (0, 1), (-1, 2), (1, 0), (0, 2), (-1, 3), (1, 1), (0, 3), (1, 2), (2, 0),
-    (1, 3), (2, 1), (3, 0), (2, 2), (3, 1), (2, 3), (3, 2), (4, 0), (3, 3), (4, 1), (5, 0), (4, 2),
-    (6, 0), (4, 3), (5, 1), (5, 2), (6, 1), (5, 3), (6, 2), (6, 3),
+    (-1, 0), (0, 0), (-1, 1), (0, 1), (-1, 2), (0, 2), (1, 0), (-1, 3), (0, 3), (1, 1), (1, 2), (2, 0),
+    (1, 3), (2, 1), (3, 0), (2, 2), (3, 1), (2, 3), (3, 2), (4, 0), (3, 3), (4, 1), (4, 2), (4, 3),
+    (5, 0), (5, 2), (5, 1), (5, 3), (6, 0), (6, 1), (6, 2), (6, 3),
 )
 COPIES = 3 + 7 + 3 + 7 + 3 + 4
 FAR = 2

time: 71.7 us -> 71.1 us (level)
  no operation moved by 1% of the time
where the time goes in v4:
time: 71.1 us; the launch traced here: 71 us
  Pallas kernels  71 us (100%)
    pallas_call x1, Pallas kernels, tensor_call(): pl.pallas_call(tensor_kernel, out_shape=jax.ShapeDtypeStruct((2, ROWS, M)...  67.6 us
    pallas_call x1, Pallas kernels, widen_call(): pl.pallas_call(widen_kernel, out_shape=jax.ShapeDtypeStruct((M * M, M), F...  3.45 us

profile of v4, /device:TPU:1, one launch (start us, length us, event | category | flops | bytes accessed | tf_op | source)
XLA Modules:
  0.0 71.0 jit_solution(3192084573223651917)
XLA Ops:
  0.0 67.6 %tensor.1 = bf16[2,8192,128]{2,1,0:T(8,128)(2,1)S(1)} custom-call(bf16[2,10,3,8,128]{4,3,2,1,0:T(8,128)(2,1)} %bitcast.4, f32[2,8,10]{2,1,0:T(8,128)} %w_hbm.1), custom_call_target="tpu_custom_call" | custom-call | tf_op jit(solution)/shard_map/tensor/pallas_call | solution.py:355
  67.6 3.5 %widen.1 = f32[16384,128]{1,0:T(8,128)} custom-call(bf16[16384,128]{1,0:T(8,128)(2,1)S(1)} %bitcast.3), custom_call_target="tpu_custom_call" | custom-call | tf_op jit(solution)/shard_map/widen/pallas_call | solution.py:406
